TPU v7x, 512 devices: a whole 4x4x16 slice. The times are simulated.
512 devices in a mesh: section: 4 (over x), seq: 16 (over y, z_lo), wide: 8 (over z_hi, core).
Axes of the slice: x: 4, y: 4, z: 16 (z_hi: 4, z_lo: 4; z = z_hi * 4 + z_lo), core: 2. Of those that a mesh axis runs over, the one named last changes fastest.
Arguments:
- q_self: bfloat16 [4, 4096, 5120], P('section', 'seq', 'wide'), may hold values from -6 to 6
- k_self: bfloat16 [4, 4096, 5120], P('section', 'seq', 'wide'), may hold values from -6 to 6
- v_self: bfloat16 [4, 4096, 5120], P('section', 'seq', 'wide'), may hold values from -6 to 6
- gain_q_self: float32 [5120], P('wide'), may hold values from 1.2 to 2.4
- gain_k_self: float32 [5120], P('wide'), may hold values from 1.2 to 2.4
- counts: int32 [4], replicated, may hold values from 1 to 4096, 12288 in all
- q_cross: bfloat16 [4, 4096, 5120], P('section', 'seq', 'wide'), may hold values from -6 to 6
- cap_kv: bfloat16 [2, 4, 512, 5120], P(None, 'section', 'seq', 'wide'), may hold values from -6 to 6
- gain_q_cross: float32 [5120], P('wide'), may hold values from 1.2 to 2.4
- gain_k_cross: float32 [5120], P('wide'), may hold values from 1.2 to 2.4
- cap_len: int32 [4], replicated, may hold values from 1 to 512, 1024 in all
- owner: int32 [4], replicated, may hold values from 0 to 3, each once
Outputs:
- out_self: bfloat16 [4, 4096, 5120], P('section', 'seq', 'wide')
- out_cross: bfloat16 [4, 4096, 5120], P('section', 'seq', 'wide')
Inputs may be any that keep to these rules, and one draw needn't show every extreme that they name: owner is a permutation of the clips.
All inputs are finite; a program needn't handle non-finite values.
Results may differ from a plain program's by a relative error of at most 0.012.
The roundings to bfloat16 on the way count: a program that leaves them out, or rounds other values in their place, can miss the bound.
Values may be sent and summed in bfloat16 or wider, within the bound.
A program may use at most 128 MiB of HBM per device.

v0:
```python
import math
import jax
import jax.numpy as jnp
from jax import lax
from jax.sharding import PartitionSpec as P

D = 5120
HEAD = 128
masked_score = -1e30


def square_sums(values):
    floats = values.astype(jnp.float32)
    return jnp.sum(floats * floats, axis=-1)


def scaled_rows(values, total_squares, gain):
    floats = values.astype(jnp.float32)
    factor = lax.rsqrt(total_squares / D + 1e-06)
    return (floats * factor[:, None] * gain[None, :]).astype(jnp.bfloat16)


def start_state(heads_here, rows):
    running = jnp.full((heads_here, rows), masked_score, jnp.float32)
    totals = jnp.zeros((heads_here, rows), jnp.float32)
    accum = jnp.zeros((heads_here, rows, HEAD), jnp.float32)
    return (running, totals, accum)


def attend_rows(state, queries, keys, values, limit):
    heads_here = queries.shape[1]
    count_rows = keys.shape[0]
    block_rows = math.gcd(count_rows, 512)
    blocks = count_rows // block_rows
    key_blocks = keys.reshape(blocks, block_rows, heads_here, HEAD)
    value_blocks = values.reshape(blocks, block_rows, heads_here, HEAD)
    factor = 1.0 / math.sqrt(HEAD)

    def one_block(carry, inputs):
        running, totals, accum = carry
        key_block, value_block, number = inputs
        scores = (
            jnp.einsum("qhd,khd->hqk", queries, key_block, preferred_element_type=jnp.float32)
            * factor
        )
        position = number * block_rows + jnp.arange(block_rows, dtype=jnp.int32)
        scores = jnp.where((position < limit)[None, None, :], scores, masked_score)
        newest = jnp.maximum(running, jnp.max(scores, axis=-1))
        rescale = jnp.exp(running - newest)
        weights = jnp.exp(scores - newest[:, :, None])
        totals = totals * rescale + jnp.sum(weights, axis=-1)
        update = jnp.einsum(
            "hqk,khd->hqd",
            weights.astype(jnp.bfloat16),
            value_block,
            preferred_element_type=jnp.float32,
        )
        accum = accum * rescale[:, :, None] + update
        return ((newest, totals, accum), None)

    numbers = jnp.arange(blocks, dtype=jnp.int32)
    state, unused = lax.scan(one_block, state, (key_blocks, value_blocks, numbers))
    return state


def finish(state):
    running, totals, accum = state
    result = accum / totals[:, :, None]
    heads_here, rows, width = result.shape
    return result.transpose(1, 0, 2).reshape(rows, heads_here * width).astype(jnp.bfloat16)[None]


def per_device(
    q_self,
    k_self,
    v_self,
    gain_q_self,
    gain_k_self,
    counts,
    q_cross,
    cap_kv,
    gain_q_cross,
    gain_k_cross,
    cap_len,
    owner,
):
    rows = q_self.shape[1]
    heads_here = q_self.shape[2] // HEAD
    section_index = lax.axis_index("section")
    section_count = lax.axis_size("section")
    latent_count = lax.dynamic_index_in_dim(counts, section_index, 0, keepdims=False)
    totals = lax.psum(
        (square_sums(q_self[0]), square_sums(k_self[0]), square_sums(q_cross[0])), "wide"
    )
    q_hat = scaled_rows(q_self[0], totals[0], gain_q_self).reshape(rows, heads_here, HEAD)
    k_hat = scaled_rows(k_self[0], totals[1], gain_k_self)
    cross_hat = scaled_rows(q_cross[0], totals[2], gain_q_cross).reshape(rows, heads_here, HEAD)
    keys = lax.all_gather(k_hat[None], "seq", axis=1, tiled=True)
    values = lax.all_gather(v_self, "seq", axis=1, tiled=True)
    count_rows = keys.shape[1]
    self_state = attend_rows(
        start_state(heads_here, rows),
        q_hat,
        keys[0].reshape(count_rows, heads_here, HEAD),
        values[0].reshape(count_rows, heads_here, HEAD),
        latent_count,
    )
    out_self = finish(self_state)
    section_numbers = jnp.arange(section_count, dtype=jnp.int32)
    source = jnp.sum(jnp.where(owner == section_index, section_numbers, 0))
    caption_length = lax.dynamic_index_in_dim(cap_len, source, 0, keepdims=False)
    whole = lax.all_gather(cap_kv, "seq", axis=2, tiled=True)
    key_totals = lax.psum(square_sums(whole[0, 0]), "wide")
    own_keys = scaled_rows(whole[0, 0], key_totals, gain_k_cross)
    assembled = jnp.stack([own_keys, whole[1, 0]])[:, None]
    routed = lax.all_gather(assembled, "section", axis=1, tiled=True)
    chosen = lax.dynamic_index_in_dim(routed, source, 1, keepdims=False)
    count_rows = chosen.shape[1]
    cross_state = attend_rows(
        start_state(heads_here, rows),
        cross_hat,
        chosen[0].reshape(count_rows, heads_here, HEAD),
        chosen[1].reshape(count_rows, heads_here, HEAD),
        caption_length,
    )
    out_cross = finish(cross_state)
    return (out_self, out_cross)


def solution(mesh):
    return jax.shard_map(
        per_device,
        mesh=mesh,
        in_specs=(
            P("section", "seq", "wide"),
            P("section", "seq", "wide"),
            P("section", "seq", "wide"),
            P("wide"),
            P("wide"),
            P(),
            P("section", "seq", "wide"),
            P(None, "section", "seq", "wide"),
            P("wide"),
            P("wide"),
            P(),
            P(),
        ),
        out_specs=(P("section", "seq", "wide"), P("section", "seq", "wide")),
        check_vma=False,
    )
```

profile of v0, /device:TPU:1, one launch (start us, length us, event | category | flops | bytes accessed | tf_op | source)
XLA Modules:
  0.0 517.4 jit_solution(16021521661886454871)
XLA Ops:
  12.3 82.7 %all-gather.10.cloned.1.call-done = bf16[2,1,512,640]{3,2,1,0:T(8,128)(2,1)} async-done(((bf16[2,1,32,640]{3,2,1,0:T(8,128)(2,1)}), bf16[2,1,512,640]{3,2,1,0:T(8,128)(2,1)}) %all-gather.10.cloned.1.call-update) | async-done | bytes 1310736 | tf_op jit(solution)/shard_map/all_gather | solution.py:112
  95.1 1.3 fusion.28
  96.4 27.6 %all-reduce = (f32[256]{0:T(256)S(1)}, f32[256]{0:T(256)S(1)}, f32[512]{0:T(512)S(1)}, f32[256]{0:T(256)S(1)}) all-reduce(f32[256]{0:T(256)S(1)} %fusion.47, f32[256]{0:T(256)S(1)} %multiply_reduce_fusion.1, f32[512]{0:T(512)S(1)} %fusion.28, f32[256]{0:T(256)S(1)} %multiply_reduce_fusion), channel_id=1, replica_groups=mesh['section'=4,'seq'=16,'wide'=8] {'wide'}, use_global_device_ids=true, to_apply=%region_1.2 | all-reduce | flops 1280 | bytes 10240 | tf_op jit(solution)/shard_map/psum | solution.py:92
  124.0 1.1 slice_bitcast_fusion
  125.2 1.4 fusion.27
  126.6 1.3 pad_maximum_fusion
  133.7 98.9 %all-gather.8.cloned.1.call-done = bf16[1,4096,640]{2,1,0:T(8,128)(2,1)} async-done(((bf16[1,256,640]{2,1,0:T(8,128)(2,1)}), bf16[1,4096,640]{2,1,0:T(8,128)(2,1)}) %all-gather.8.cloned.1.call-update) | async-done | bytes 5242896 | tf_op jit(solution)/shard_map/all_gather | solution.py:99
  232.6 12.6 %reshape.180 = bf16[8,512,5,128]{3,2,1,0:T(8,128)(2,1)} reshape(bf16[1,4096,640]{2,1,0:T(8,128)(2,1)} %all-gather.8.cloned.1.call-done) | data formatting | bytes 10485760 | tf_op jit(solution)/shard_map/reshape;reshape;squeeze | solution.py:36
  245.3 7.2 %copy.38 = bf16[8,512,5,128]{3,1,2,0:T(8,128)(2,1)} copy(bf16[8,512,5,128]{3,2,1,0:T(8,128)(2,1)} %reshape.180) | data formatting | bytes 10485760
  252.5 44.5 %all-gather.12.cloned.1.call-done = bf16[2,2048,640]{2,1,0:T(8,128)(2,1)} async-done(((bf16[2,512,640]{2,1,0:T(8,128)(2,1)}), bf16[2,2048,640]{2,1,0:T(8,128)(2,1)}) %all-gather.12.cloned.1.call-update) | async-done | bytes 5242896 | tf_op jit(solution)/shard_map/all_gather | solution.py:116
  297.0 1.4 constant_dynamic-slice_fusion
  302.5 125.5 %all-gather.6.cloned.1.call-done = bf16[1,4096,640]{2,1,0:T(8,128)(2,1)} async-done(((bf16[1,256,640]{2,1,0:T(8,128)(2,1)}), bf16[1,4096,640]{2,1,0:T(8,128)(2,1)}) %all-gather.6.cloned.1.call-update) | async-done | bytes 5242896 | tf_op jit(solution)/shard_map/all_gather | solution.py:98
  428.0 12.6 %reshape.179 = bf16[8,512,5,128]{3,2,1,0:T(8,128)(2,1)} reshape(bf16[1,4096,640]{2,1,0:T(8,128)(2,1)} %all-gather.6.cloned.1.call-done) | data formatting | bytes 10485760 | tf_op jit(solution)/shard_map/reshape;reshape;squeeze | solution.py:35
  440.6 7.1 %copy.36 = bf16[8,512,5,128]{3,1,2,0:T(8,128)(2,1)} copy(bf16[8,512,5,128]{3,2,1,0:T(8,128)(2,1)} %reshape.179) | data formatting | bytes 10485760
  447.8 60.8 %while.3 = (s32[]{:T(128)}, f32[5,256]{1,0:T(8,128)S(1)}, f32[5,256]{1,0:T(8,128)S(1)}, f32[5,256,128]{2,1,0:T(8,128)}, s32[8]{0:T(128)S(1)}, /*index=5*/s32[]{:...) while((s32[]{:T(128)}, f32[5,256]{1,0:T(8,128)S(1)}, ...), condition=%wide.region_7.8_spmd.clone, body=%wide.region_4.7_spmd.clone.sunk | while | flops 343252224 | bytes 16141529 | solution.py:62
  449.5 1.6 bitcast_reduce_fusion.2
  452.3 2.1 fusion.71
  457.1 1.6 bitcast_reduce_fusion.2
  459.9 2.1 fusion.71
  464.8 1.6 bitcast_reduce_fusion.2
  467.5 2.1 fusion.71
  472.4 1.6 bitcast_reduce_fusion.2
  475.1 2.1 fusion.71
  480.0 1.6 bitcast_reduce_fusion.2
  482.7 2.1 fusion.71
  487.6 1.6 bitcast_reduce_fusion.2
  490.3 2.1 fusion.71
  495.2 1.6 bitcast_reduce_fusion.2
  497.9 2.1 fusion.71
  502.8 1.6 bitcast_reduce_fusion.2
  505.5 2.1 fusion.71
  508.6 1.3 copy.39
  (133 shorter events, 38.6 us)
Async XLA Ops:
  7.2 118.0 %copy-start.3 = (f32[640]{0:T(1024)S(1)}, f32[640]{0:T(1024)}, u32[]{:S(2)}) copy-start(f32[640]{0:T(1024)} %param.23) | copy-start | bytes 7684
  7.2 87.9 %all-gather.10.cloned.1.call-start = ((), (), s32[]{:S(2)}) async-start(), calls=%async_computation.2 | async-start | bytes 1392640 | tf_op jit(solution)/shard_map/all_gather | solution.py:112
  7.9 224.7 %all-gather.8.cloned.1.call-start = ((), (), s32[]{:S(2)}) async-start(), calls=%async_computation.1 | async-start | bytes 5570560 | tf_op jit(solution)/shard_map/all_gather | solution.py:99
  8.7 288.4 %all-gather.12.cloned.1.call-start = ((), (), s32[]{:S(2)}) async-start(), calls=%async_computation.3 | async-start | bytes 6553600 | tf_op jit(solution)/shard_map/all_gather | solution.py:116
  125.2 2.8 copy-start
  125.2 2.8 copy-start.4
  126.6 2.3 copy-start.7
  126.6 4.9 copy-start.8
  126.6 5.5 %copy-start.9 = (s32[4]{0:T(128)S(1)}, s32[4]{0:T(128)}, u32[]{:S(2)}) copy-start(s32[4]{0:T(128)} %param.19) | copy-start | bytes 52
  126.6 6.7 %copy-start.5 = (f32[640]{0:T(1024)S(1)}, f32[640]{0:T(1024)}, u32[]{:S(2)}) copy-start(f32[640]{0:T(1024)} %param.17) | copy-start | bytes 7684
  127.9 300.1 %all-gather.6.cloned.1.call-start = ((), (), s32[]{:S(2)}) async-start(), calls=%async_computation | async-start | bytes 5570560 | tf_op jit(solution)/shard_map/all_gather | solution.py:98
  297.0 1.9 copy-start.6
  451.2 1.1 copy-start.1
  454.4 0.9 copy-start.2
  458.8 1.1 copy-start.1
  462.0 0.9 copy-start.2
  466.4 1.1 copy-start.1
  469.7 0.9 copy-start.2
  474.0 1.1 copy-start.1
  477.3 0.9 copy-start.2
  481.6 1.1 copy-start.1
  484.9 0.9 copy-start.2
  489.2 1.1 copy-start.1
  492.5 0.9 copy-start.2
  496.8 1.1 copy-start.1
  500.1 0.9 copy-start.2
  504.4 1.1 copy-start.1
  507.7 0.9 copy-start.2
Sparse Core Ops, SparseCore 0:
  10.1 84.9 all-gather.9
  97.1 135.4 all-gather.7
  234.7 62.2 all-gather.11
  299.5 128.4 all-gather.5
where the time goes:
time: 520 us; the launch traced here: 517 us
  waiting for transfers between devices  353 us (68%)
  local copies, waits for them, and re-layouts  64.9 us (12%)
  matrix products  32.1 us (6%)
  blocking collectives  27.6 us (5%)
  other arithmetic  17.7 us (3%)
  between operations  16 us (3%)
  loops' own time  5.74 us (1%)
    all_gather x1, waiting for transfers between devices, per_device(): keys = lax.all_gather(k_hat[None], 'seq', axis=1, tiled=True)  126 us
    all_gather x1, waiting for transfers between devices, per_device(): values = lax.all_gather(v_self, 'seq', axis=1, tiled=True)  98.9 us
    all_gather x1, waiting for transfers between devices, per_device(): whole = lax.all_gather(cap_kv, 'seq', axis=2, tiled=True)  82.7 us
    all_gather x1, waiting for transfers between devices, per_device(): routed = lax.all_gather(assembled, 'section', axis=1, tiled=True)  44.5 us
    psum x1, blocking collectives, per_device(): lax.psum((square_sums(q_self[0]), square_sums(k_self[0]), square_sums(q_c...  27.6 us
    unnamed x23, local copies, waits for them, and re-layouts  18.7 us
    dot_general x9, matrix products, one_block(): jnp.einsum('hqk,khd->hqd', weights.astype(jnp.bfloat16), value_block, pre...  18 us
    dot_general x9, matrix products, one_block(): jnp.einsum('qhd,khd->hqk', queries, key_block, preferred_element_type=jnp...  14.2 us
  transfers between devices with their start and end apart: 4, of which 4 were waited for; matrix products, arithmetic and copies ran while one was open for 7% of the time, Pallas kernels for 0%

commit v1 on v0

--- a/solution.py
+++ b/solution.py
@@ -113,7 +113,8 @@
     key_totals = lax.psum(square_sums(whole[0, 0]), "wide")
     own_keys = scaled_rows(whole[0, 0], key_totals, gain_k_cross)
     assembled = jnp.stack([own_keys, whole[1, 0]])[:, None]
-    routed = lax.all_gather(assembled, "section", axis=1, tiled=True)
+    copies = jnp.concatenate([assembled] * lax.axis_size("section"), axis=1)
+    routed = lax.all_to_all(copies, "section", 1, 1, tiled=True)
     chosen = lax.dynamic_index_in_dim(routed, source, 1, keepdims=False)
     count_rows = chosen.shape[1]
     cross_state = attend_rows(

time: 520 us -> 453 us (0.87)
  waiting for transfers between devices: 353 us -> 280 us
    all_gather x1, waiting for transfers between devices: 98.9 us -> 32.8 us  [per_device(): values = lax.all_gather(v_self, 'seq', axis=1, tiled=True)]
    all_to_all x0 -> x1, waiting for transfers between devices: none -> 54.8 us  [per_device(): routed = lax.all_to_all(copies, 'section', 1, 1, tiled=True)]
    all_gather x1 -> x0, waiting for transfers between devices: 44.5 us -> none  [per_device(): routed = lax.all_gather(assembled, 'section', axis=1, tiled=True)]
    all_gather x1, waiting for transfers between devices: 126 us -> 108 us  [per_device(): keys = lax.all_gather(k_hat[None], 'seq', axis=1, tiled=True)]
    unnamed x23 -> x25, local copies, waits for them, and re-layouts: 18.7 us -> 18.7 us
  transfers between devices with their start and end apart: 4 -> 4, of which waited for: 4 -> 4; matrix products, arithmetic and copies ran while one was open for 7% -> 9% of each run, Pallas kernels for 0% -> 0%
where the time goes in v1:
time: 453 us; the launch traced here: 451 us
  waiting for transfers between devices  280 us (62%)
  local copies, waits for them, and re-layouts  67.4 us (15%)
  matrix products  32.2 us (7%)
  blocking collectives  27.6 us (6%)
  other arithmetic  16.3 us (4%)
  between operations  16 us (4%)
  loops' own time  5.74 us (1%)
  starting transfers between devices  5.3 us (1%)
    all_gather x1, waiting for transfers between devices, per_device(): keys = lax.all_gather(k_hat[None], 'seq', axis=1, tiled=True)  108 us
    all_gather x1, waiting for transfers between devices, per_device(): whole = lax.all_gather(cap_kv, 'seq', axis=2, tiled=True)  82.7 us
    all_to_all x1, waiting for transfers between devices, per_device(): routed = lax.all_to_all(copies, 'section', 1, 1, tiled=True)  54.8 us
    all_gather x1, waiting for transfers between devices, per_device(): values = lax.all_gather(v_self, 'seq', axis=1, tiled=True)  32.8 us
    psum x1, blocking collectives, per_device(): lax.psum((square_sums(q_self[0]), square_sums(k_self[0]), square_sums(q_c...  27.6 us
    unnamed x25, local copies, waits for them, and re-layouts  18.7 us
    dot_general x9, matrix products, one_block(): jnp.einsum('hqk,khd->hqd', weights.astype(jnp.bfloat16), value_block, pre...  18 us
    dot_general x9, matrix products, one_block(): jnp.einsum('qhd,khd->hqk', queries, key_block, preferred_element_type=jnp...  14.2 us
  transfers between devices with their start and end apart: 4, of which 4 were waited for; matrix products, arithmetic and copies ran while one was open for 9% of the time, Pallas kernels for 0%

profile of v1, /device:TPU:1, one launch (start us, length us, event | category | flops | bytes accessed | tf_op | source)
XLA Modules:
  0.0 450.5 jit_solution(1514880534677432108)
XLA Ops:
  12.4 82.7 %all-gather.8.cloned.1.call-done = bf16[2,1,512,640]{3,2,1,0:T(8,128)(2,1)} async-done(((bf16[2,1,32,640]{3,2,1,0:T(8,128)(2,1)}), bf16[2,1,512,640]{3,2,1,0:T(8,128)(2,1)}) %all-gather.8.cloned.1.call-update) | async-done | bytes 1310736 | tf_op jit(solution)/shard_map/all_gather | solution.py:112
  95.1 1.4 fusion.28
  96.5 27.6 %all-reduce = (f32[256]{0:T(256)S(1)}, f32[256]{0:T(256)S(1)}, f32[512]{0:T(512)S(1)}, f32[256]{0:T(256)S(1)}) all-reduce(f32[256]{0:T(256)S(1)} %fusion.47, f32[256]{0:T(256)S(1)} %multiply_reduce_fusion.1, f32[512]{0:T(512)S(1)} %fusion.28, f32[256]{0:T(256)S(1)} %multiply_reduce_fusion), channel_id=1, replica_groups=mesh['section'=4,'seq'=16,'wide'=8] {'wide'}, use_global_device_ids=true, to_apply=%region_1.2 | all-reduce | flops 1280 | bytes 10240 | tf_op jit(solution)/shard_map/psum | solution.py:92
  125.1 1.1 slice_bitcast_fusion
  127.3 2.8 concatenate.3
  130.0 5.2 %all-to-all-start = ((bf16[2,4,512,640]{2,3,0,1:T(8,128)(2,1)}), bf16[2,4,512,640]{2,3,0,1:T(8,128)(2,1)}, u32[]{:S(2)}, u32[]{:S(2)}) async-start(bf16[2,4,512,640]{2,3,0,1:T(8,128)(2,1)} %concatenate.3), calls=%async_computation | async-start | bytes 10485760 | tf_op jit(solution)/shard_map/all_to_all | solution.py:117
  140.1 54.8 %all-to-all-done = bf16[2,4,512,640]{2,3,0,1:T(8,128)(2,1)} async-done(((bf16[2,4,512,640]{2,3,0,1:T(8,128)(2,1)}), bf16[2,4,512,640]{2,3,0,1:T(8,128)(2,1)}, u32[]{:S(2)}, u32[]{:S(2)}) %all-to-all-start) | async-done | bytes 5242912 | tf_op jit(solution)/shard_map/all_to_all | solution.py:117
  194.9 1.4 constant_dynamic-slice_fusion
  199.8 32.8 %all-gather.6.cloned.1.call-done = bf16[1,4096,640]{2,1,0:T(8,128)(2,1)} async-done(((bf16[1,256,640]{2,1,0:T(8,128)(2,1)}), bf16[1,4096,640]{2,1,0:T(8,128)(2,1)}) %all-gather.6.cloned.1.call-update) | async-done | bytes 5242896 | tf_op jit(solution)/shard_map/all_gather | solution.py:99
  232.6 12.6 %reshape.181 = bf16[8,512,5,128]{3,2,1,0:T(8,128)(2,1)} reshape(bf16[1,4096,640]{2,1,0:T(8,128)(2,1)} %all-gather.6.cloned.1.call-done) | data formatting | bytes 10485760 | tf_op jit(solution)/shard_map/reshape;reshape;squeeze | solution.py:36
  245.3 7.2 %copy.39 = bf16[8,512,5,128]{3,1,2,0:T(8,128)(2,1)} copy(bf16[8,512,5,128]{3,2,1,0:T(8,128)(2,1)} %reshape.181) | data formatting | bytes 10485760
  252.4 108.4 %all-gather.4.cloned.1.call-done = bf16[1,4096,640]{2,1,0:T(8,128)(2,1)} async-done(((bf16[1,256,640]{2,1,0:T(8,128)(2,1)}), bf16[1,4096,640]{2,1,0:T(8,128)(2,1)}) %all-gather.4.cloned.1.call-update) | async-done | bytes 5242896 | tf_op jit(solution)/shard_map/all_gather | solution.py:98
  360.8 12.6 %reshape.180 = bf16[8,512,5,128]{3,2,1,0:T(8,128)(2,1)} reshape(bf16[1,4096,640]{2,1,0:T(8,128)(2,1)} %all-gather.4.cloned.1.call-done) | data formatting | bytes 10485760 | tf_op jit(solution)/shard_map/reshape;reshape;squeeze | solution.py:35
  373.4 7.2 %copy.37 = bf16[8,512,5,128]{3,1,2,0:T(8,128)(2,1)} copy(bf16[8,512,5,128]{3,2,1,0:T(8,128)(2,1)} %reshape.180) | data formatting | bytes 10485760
  380.7 61.1 %while.3 = (s32[]{:T(128)}, f32[5,256]{1,0:T(8,128)S(1)}, f32[5,256]{1,0:T(8,128)S(1)}, f32[5,256,128]{2,1,0:T(8,128)}, s32[8]{0:T(128)S(1)}, /*index=5*/s32[]{:...) while((s32[]{:T(128)}, f32[5,256]{1,0:T(8,128)S(1)}, ...), condition=%wide.region_7.8_spmd.clone, body=%wide.region_4.7_spmd.clone.sunk | while | flops 343252224 | bytes 16141529 | solution.py:62
  382.5 1.6 bitcast_reduce_fusion.2
  385.3 2.1 fusion.71
  390.2 1.6 bitcast_reduce_fusion.2
  392.9 2.1 fusion.71
  397.8 1.6 bitcast_reduce_fusion.2
  400.5 2.1 fusion.71
  405.4 1.6 bitcast_reduce_fusion.2
  408.2 2.1 fusion.71
  413.1 1.7 bitcast_reduce_fusion.2
  415.8 2.1 fusion.71
  420.7 1.6 bitcast_reduce_fusion.2
  423.4 2.1 fusion.71
  428.3 1.6 bitcast_reduce_fusion.2
  431.1 2.1 fusion.71
  436.0 1.6 bitcast_reduce_fusion.2
  438.7 2.1 fusion.71
  441.7 1.3 copy.40
  (134 shorter events, 39.4 us)
Async XLA Ops:
  7.2 117.0 %copy-start.1 = (bf16[1,256,640]{2,1,0:T(8,128)(2,1)S(1)}, bf16[1,256,640]{2,1,0:T(8,128)(2,1)}, u32[]{:S(2)}) copy-start(bf16[1,256,640]{2,1,0:T(8,128)(2,1)} %param.15) | copy-start | bytes 983044
  7.2 117.0 %copy-start.4 = (f32[640]{0:T(1024)S(1)}, f32[640]{0:T(1024)}, u32[]{:S(2)}) copy-start(f32[640]{0:T(1024)} %param.18) | copy-start | bytes 7684
  7.2 87.9 %all-gather.8.cloned.1.call-start = ((), (), s32[]{:S(2)}) async-start(), calls=%async_computation.3 | async-start | bytes 1392640 | tf_op jit(solution)/shard_map/all_gather | solution.py:112
  7.9 224.7 %all-gather.6.cloned.1.call-start = ((), (), s32[]{:S(2)}) async-start(), calls=%async_computation.2 | async-start | bytes 5570560 | tf_op jit(solution)/shard_map/all_gather | solution.py:99
  8.7 117.5 %copy-start.5 = (f32[640]{0:T(1024)S(1)}, f32[640]{0:T(1024)}, u32[]{:S(2)}) copy-start(f32[640]{0:T(1024)} %param.23) | copy-start | bytes 7684
  8.7 352.1 %all-gather.4.cloned.1.call-start = ((), (), s32[]{:S(2)}) async-start(), calls=%async_computation.1 | async-start | bytes 5570560 | tf_op jit(solution)/shard_map/all_gather | solution.py:98
  95.1 31.1 %copy-start = (bf16[2,1,512,640]{3,2,1,0:T(8,128)(2,1)S(1)}, bf16[2,1,512,640]{3,2,1,0:T(8,128)(2,1)}, u32[]{:S(2)}) copy-start(bf16[2,1,512,640]{3,2,1,0:T(8,128)(2,1)} %all-gather.8.cloned.1.call-done) | copy-start | bytes 3932164
  130.0 5.2 %copy-start.8 = (s32[4]{0:T(128)S(1)}, s32[4]{0:T(128)}, u32[]{:S(2)}) copy-start(s32[4]{0:T(128)} %param.25) | copy-start | bytes 52
  130.0 7.8 %copy-start.9 = (s32[4]{0:T(128)S(1)}, s32[4]{0:T(128)}, u32[]{:S(2)}) copy-start(s32[4]{0:T(128)} %param.24) | copy-start | bytes 52
  130.0 8.4 %copy-start.10 = (s32[4]{0:T(128)S(1)}, s32[4]{0:T(128)}, u32[]{:S(2)}) copy-start(s32[4]{0:T(128)} %param.19) | copy-start | bytes 52
  130.0 9.7 %copy-start.6 = (f32[640]{0:T(1024)S(1)}, f32[640]{0:T(1024)}, u32[]{:S(2)}) copy-start(f32[640]{0:T(1024)} %param.17) | copy-start | bytes 7684
  130.0 64.9 %all-to-all-start = ((bf16[2,4,512,640]{2,3,0,1:T(8,128)(2,1)}), bf16[2,4,512,640]{2,3,0,1:T(8,128)(2,1)}, u32[]{:S(2)}, u32[]{:S(2)}) async-start(bf16[2,4,512,640]{2,3,0,1:T(8,128)(2,1)} %concatenate.3), calls=%async_computation | async-start | bytes 10485760 | tf_op jit(solution)/shard_map/all_to_all | solution.py:117
  135.2 61.0 %copy-start.7 = (f32[640]{0:T(1024)S(1)}, f32[640]{0:T(1024)}, u32[]{:S(2)}) copy-start(f32[640]{0:T(1024)} %param.22) | copy-start | bytes 7684
  384.2 1.1 copy-start.2
  387.4 0.8 copy-start.3
  391.8 1.1 copy-start.2
  395.1 0.8 copy-start.3
  399.5 1.1 copy-start.2
  402.7 0.8 copy-start.3
  407.1 1.1 copy-start.2
  410.3 0.8 copy-start.3
  414.7 1.1 copy-start.2
  418.0 0.8 copy-start.3
  422.4 1.1 copy-start.2
  425.6 0.8 copy-start.3
  430.0 1.1 copy-start.2
  433.2 0.8 copy-start.3
  437.6 1.1 copy-start.2
  440.9 0.8 copy-start.3
Sparse Core Ops, SparseCore 0:
  10.1 84.9 all-gather.7
  97.2 135.4 all-gather.5
  235.3 125.4 all-gather.3
